TPU v7x, 32 devices: a whole 2x2x4 slice. The times are simulated.
32 devices in a mesh: block: 4 (over y, core), row: 8 (over z, x).
Axes of the slice: x: 2, y: 2, z: 4, core: 2. Of those that a mesh axis runs over, the one named last changes fastest.
Arguments:
- snapshots: bfloat16 [16384, 1024], P('block', 'row'), may hold values from -6 to 6
- usable_frame_tallies: int32 [64], replicated, may hold values from 64 to 256, as said below
- retained_frequency_slots: int32 [64], replicated, may hold values from 0 to 127, as said below
- modes: bfloat16 [64, 2, 1024, 512], P('block', None, 'row'), may hold values from -0.125 to 0.125
Outputs:
- coefficients: float32 [64, 2, 64, 512], P('row', None, 'block')
- energy: float32 [64, 512], P('block')
Inputs may be any that keep to these rules, and one draw needn't show every extreme that they name: Only the first usable_frame_tallies[b] snapshots of block b are valid; some block is full. `retained_frequency_slots`: 64 distinct bins in increasing order; bin 0 and bin 256 // 2 - 1 are always kept.
All inputs are finite; a program needn't handle non-finite values.
Results may differ from a plain program's by a relative error of at most 0.004.
Values may be sent and summed in bfloat16 or wider, within the bound.
A program may use at most 64 MiB of HBM per device.

v0:
```python
import functools

import jax
import jax.numpy as jnp
from jax import lax
from jax.experimental import pallas as pl
from jax.experimental.pallas import tpu as pltpu
from jax.sharding import PartitionSpec as P

FRAMES_PER_SEG = 256
MESH = pl.DeviceIdType.MESH
F32 = jnp.float32
BF16 = jnp.bfloat16
SWAPPED = (1, 3, 5)
AHEAD = 3
SENT_AHEAD = 10
LANES = 128


def sin_poly(x):
    y = x * x
    s = 1.0 / 6227020800.0
    for c in (-1.0 / 39916800.0, 1.0 / 362880.0, -1.0 / 5040.0, 1.0 / 120.0, -1.0 / 6.0, 1.0):
        s = s * y + c
    return x * s


def cos_poly(x):
    y = x * x
    s = 1.0 / 479001600.0
    for c in (-1.0 / 3628800.0, 1.0 / 40320.0, -1.0 / 720.0, 1.0 / 24.0, -0.5, 1.0):
        s = s * y + c
    return s


def kernel(
    dims,
    tally_ref,
    slot_ref,
    snap_hbm,
    modes_hbm,
    out_ref,
    energy_ref,
    snap,
    modes,
    prod,
    trig,
    wide,
    spec,
    arrived,
    full,
    efull,
    load_sem,
    a_send,
    a_recv,
    r_send,
    r_recv,
    e_send,
    e_recv,
    *stages,
):
    nb, nr, spans, groups, orders = dims
    chunks = len(spans)
    bits = nr.bit_length() - 1
    sends, recvs, eparts = stages[:bits], stages[bits : 2 * bits], stages[2 * bits :]
    frames = FRAMES_PER_SEG
    slots = slot_ref.shape[0]
    blocks = tally_ref.shape[0]
    own_blocks = blocks // nb
    kl = slots // nb
    share = blocks // nr
    m = modes_hbm.shape[3]
    me_b = lax.axis_index("block")
    me_r = lax.axis_index("row")
    mine = [(me_r // (1 << t)) % 2 for t in range(bits)]

    def peer_b(j):
        return lax.rem(me_b + j, nb)

    barrier = pltpu.get_barrier_semaphore()
    for j in range(1, nb):
        pl.semaphore_signal(barrier, inc=1, device_id=(peer_b(j), me_r), device_id_type=MESH)
    partners = [me_r + (1 - 2 * mine[t]) * (1 << t) for t in range(bits)]
    for t in range(bits):
        pl.semaphore_signal(barrier, inc=1, device_id=(me_b, partners[t]), device_id_type=MESH)
    snap_load = pltpu.make_async_copy(snap_hbm, snap, load_sem.at[0])
    snap_load.start()
    modes_load = pltpu.make_async_copy(modes_hbm, modes, load_sem.at[1])
    modes_load.start()

    times = lax.broadcasted_iota(jnp.int32, (1, frames), 1)
    for k in range(slots):
        prod[k : k + 1, :] = (slot_ref[k] * times) & (frames - 1)
    eighth = frames // 8
    turned = prod[...] + eighth
    quarter = (turned >> (eighth.bit_length())) & 3
    angle = ((turned & (2 * eighth - 1)) - eighth).astype(F32) * (2.0 * jnp.pi / frames)
    sn = sin_poly(angle)
    cs = cos_poly(angle)
    odd = (quarter & 1) == 1
    cos_mag = jnp.where(odd, sn, cs)
    sin_mag = jnp.where(odd, cs, sn)
    cos_neg = (quarter == 1) | (quarter == 2)
    trig[0:slots, :] = jnp.where(cos_neg, -cos_mag, cos_mag)
    trig[slots : 2 * slots, :] = jnp.where(quarter >= 2, sin_mag, -sin_mag)

    rows = lax.broadcasted_iota(jnp.int32, (own_blocks, frames), 0)
    cols = lax.broadcasted_iota(jnp.int32, (own_blocks, frames), 1)
    counts = jnp.zeros((own_blocks, frames), jnp.int32)
    for b in range(own_blocks):
        counts = jnp.where(rows == b, tally_ref[me_b * own_blocks + b], counts)
    at = (cols.astype(F32) + 0.5) / counts.astype(F32)
    wave = sin_poly(jnp.pi * jnp.minimum(at, 1.0 - at))
    window = jnp.where(cols < counts, wave * wave, 0.0)
    scaling = 1.0 / jnp.sqrt(jnp.sum(window * window, axis=1, keepdims=True))
    scaled = scaling * window

    snap_load.wait()
    for b in range(own_blocks):
        table = (scaled[b : b + 1, :] * trig[...]).astype(BF16)
        wide[pl.ds(b, 2 * slots, stride=own_blocks), :] = jnp.dot(
            table, snap[b * frames : (b + 1) * frames, :], preferred_element_type=F32
        )

    pl.semaphore_wait(barrier, nb - 1 + bits)

    def part_of(c):
        return pl.ds(*spans[c])

    def keys_of(c):
        return range(spans[c][0], spans[c][0] + spans[c][1])

    def a_copy(c, j):
        to = peer_b(j)
        return pltpu.make_async_remote_copy(
            src_ref=spec.at[to, part_of(c)],
            dst_ref=arrived.at[me_b, part_of(c)],
            send_sem=a_send.at[c, j - 1],
            recv_sem=a_recv.at[c, j - 1],
            device_id=(to, me_r),
            device_id_type=MESH,
        )

    def send_spectra(c):
        for p in range(nb):
            for k in keys_of(c):
                for part in range(2):
                    first = (part * slots + p * kl + k) * own_blocks
                    spec[p, k, part] = wide[first : first + own_blocks, :].astype(BF16)
        for j in range(1, nb):
            a_copy(c, j).start()
        for k in keys_of(c):
            arrived[me_b, k] = spec[me_b, k]

    for c in range(min(SENT_AHEAD, chunks)):
        send_spectra(c)

    def r_copy(c, t):
        bit = orders[c][t]
        src = sends[0].at[1 - mine[bit]] if t == 0 else sends[t]
        return pltpu.make_async_remote_copy(
            src_ref=src.at[:, part_of(c)],
            dst_ref=recvs[t].at[:, part_of(c)],
            send_sem=r_send.at[c, t],
            recv_sem=r_recv.at[c, t],
            device_id=(me_b, partners[bit]),
            device_id_type=MESH,
        )

    def row_of(c, t, q):
        order = orders[c]
        row = sum(mine[bit] * (1 << bit) for bit in order[: t + 1])
        for i, bit in enumerate(order[t + 1 :]):
            row = row + ((q // (1 << i)) % 2) * (1 << bit)
        return row

    def e_copy(h, j):
        to = lax.rem(me_r + j, nr)
        return pltpu.make_async_remote_copy(
            src_ref=eparts[h].at[me_r],
            dst_ref=eparts[h].at[me_r],
            send_sem=e_send.at[h, j - 1],
            recv_sem=e_recv.at[h, j - 1],
            device_id=(me_b, to),
            device_id_type=MESH,
        )

    def e_arrival(h, j):
        source = lax.rem(me_r + nr - j, nr)
        return pltpu.make_async_remote_copy(
            src_ref=eparts[h].at[source],
            dst_ref=eparts[h].at[source],
            send_sem=e_send.at[h, j - 1],
            recv_sem=e_recv.at[h, j - 1],
            device_id=(me_b, lax.rem(me_r + j, nr)),
            device_id_type=MESH,
        )

    def a_arrival(c, j):
        source = lax.rem(me_b + nb - j, nb)
        return pltpu.make_async_remote_copy(
            src_ref=spec.at[peer_b(j), part_of(c)],
            dst_ref=arrived.at[source, part_of(c)],
            send_sem=a_send.at[c, j - 1],
            recv_sem=a_recv.at[c, j - 1],
            device_id=(peer_b(j), me_r),
            device_id_type=MESH,
        )

    modes_load.wait()
    for c in range(chunks):
        for j in range(1, nb):
            a_arrival(c, j).wait_recv()
        if c + SENT_AHEAD < chunks:
            send_spectra(c + SENT_AHEAD)
        for k in keys_of(c):
            re = jnp.concatenate([arrived[s, k, 0] for s in range(nb)], axis=0)
            im = jnp.concatenate([arrived[s, k, 1] for s in range(nb)], axis=0)
            left = jnp.concatenate(
                [jnp.concatenate([re, im], axis=1), jnp.concatenate([im, -re], axis=1)], axis=0
            )
            right = jnp.concatenate([modes[k, 0], modes[k, 1]], axis=0)
            result = jnp.dot(left, right, preferred_element_type=F32)
            for r in range(nr):
                piece = jnp.concatenate(
                    [
                        result[r * share : (r + 1) * share],
                        result[blocks + r * share : blocks + (r + 1) * share],
                    ],
                    axis=0,
                )
                order = orders[c]
                q = sum(((r >> bit) & 1) << i for i, bit in enumerate(order[1:]))
                full[r, k] = piece
                sends[0][(r >> order[0]) & 1, q, k] = piece.astype(BF16)
        if c < AHEAD:
            r_copy(c, 0).start()

    total = tally_ref[0]
    for b in range(1, blocks):
        total = total + tally_ref[b]
    total = total.astype(F32)
    share_rows = lax.broadcasted_iota(jnp.int32, (share, 1), 0)
    weights = jnp.zeros((share, 1), F32)
    for b in range(share):
        weights = jnp.where(share_rows == b, tally_ref[me_r * share + b].astype(F32), weights)

    def finish(k, value):
        for part in range(2):
            for lane in range(m // LANES):
                out_ref[lane, pl.ds(part * kl + k, share, stride=2 * kl), :] = value[
                    part * share : (part + 1) * share, lane * LANES : (lane + 1) * LANES
                ]
        real, imag = value[:share], value[share:]
        power = weights * (real * real + imag * imag)
        efull[k : k + 1, :] = jnp.sum(power, axis=0, keepdims=True)
        for h, (first, size) in enumerate(groups):
            if k == first + size - 1:
                eparts[h][me_r] = efull[first : first + size, :].astype(BF16)
                for j in range(1, nr):
                    e_copy(h, j).start()

    def advance(c, t):
        r_copy(c, t).wait_recv()
        if t == 0 and c + AHEAD < chunks:
            r_copy(c + AHEAD, 0).start()
        if t == bits - 1:
            for k in keys_of(c):
                finish(k, full[me_r, k] + recvs[t][0, k].astype(F32))
            return
        bit = orders[c][t + 1]
        for half in range(2):
            which = mine[bit] if half else 1 - mine[bit]
            for q in range(nr >> (t + 2)):
                piece = 2 * q + which
                row = row_of(c, t, piece)
                for k in keys_of(c):
                    value = full[row, k] + recvs[t][piece, k].astype(F32)
                    if half:
                        full[row, k] = value
                    else:
                        sends[t + 1][q, k] = value.astype(BF16)
            if not half:
                r_copy(c, t + 1).start()

    for step in range(chunks + 2 * (bits - 1)):
        for t in range(bits):
            if 0 <= step - 2 * t < chunks:
                advance(step - 2 * t, t)

    for h, (first, size) in enumerate(groups):
        for j in range(1, nr):
            e_arrival(h, j).wait_recv()
        acc = eparts[h][0].astype(F32)
        for r in range(1, nr):
            acc = acc + eparts[h][r].astype(F32)
        energy_ref[first : first + size, :] = acc / total

    for c in range(chunks):
        for j in range(1, nb):
            a_copy(c, j).wait_send()
        for t in range(bits):
            r_copy(c, t).wait_send()
    for h in range(len(groups)):
        for j in range(1, nr):
            e_copy(h, j).wait_send()


def write_out(values_ref, energy_in, out_hbm, energy_out, sem):
    copies = [pltpu.make_async_copy(energy_in, energy_out, sem.at[0])]
    for lane in range(values_ref.shape[0]):
        copies.append(
            pltpu.make_async_copy(
                values_ref.at[lane],
                out_hbm.at[:, lane * LANES : (lane + 1) * LANES],
                sem.at[lane + 1],
            )
        )
    for copy in copies:
        copy.start()
    for copy in copies:
        copy.wait()


def shards(nb, nr, snapshots, usable_frame_tallies, retained_frequency_slots, modes):
    slots = retained_frequency_slots.shape[0]
    blocks = usable_frame_tallies.shape[0]
    width = snapshots.shape[1]
    kl, _, _, m = modes.shape
    own_blocks = blocks // nb
    share = blocks // nr
    bits = nr.bit_length() - 1
    singles = 0
    sizes = [2] * ((kl - singles) // 2)
    sizes += [1] * (kl - sum(sizes))
    spans = tuple((sum(sizes[:c]), sizes[c]) for c in range(len(sizes)))
    chunks = len(spans)
    plain = tuple(range(bits))
    swapped = (1, 0) + plain[2:]
    orders = tuple(swapped if c in SWAPPED else plain for c in range(chunks))
    late = kl // 2
    groups = ((0, kl - late), (kl - late, late))
    dims = (nb, nr, spans, groups, orders)
    pieces = [(nr >> (t + 1), kl, 2 * share, m) for t in range(bits)]
    dma = pltpu.SemaphoreType.DMA
    smem = pl.BlockSpec(memory_space=pltpu.SMEM)
    anywhere = pl.BlockSpec(memory_space=pl.ANY)
    vmem = pl.BlockSpec(memory_space=pltpu.VMEM)
    values, energy = pl.pallas_call(
        functools.partial(kernel, dims),
        out_shape=(
            jax.ShapeDtypeStruct((m // LANES, 2 * share * kl, LANES), F32),
            jax.ShapeDtypeStruct((kl, m), F32),
        ),
        in_specs=[smem, smem, anywhere, anywhere],
        out_specs=(vmem, vmem),
        scratch_shapes=[
            pltpu.VMEM(snapshots.shape, BF16),
            pltpu.VMEM(modes.shape, BF16),
            pltpu.VMEM((slots, FRAMES_PER_SEG), jnp.int32),
            pltpu.VMEM((2 * slots, FRAMES_PER_SEG), F32),
            pltpu.VMEM((2 * slots * own_blocks, width), F32),
            pltpu.VMEM((nb, kl, 2, own_blocks, width), BF16),
            pltpu.VMEM((nb, kl, 2, own_blocks, width), BF16),
            pltpu.VMEM((nr, kl, 2 * share, m), F32),
            pltpu.VMEM((kl, m), F32),
            dma((2,)),
            dma((chunks, nb - 1)),
            dma((chunks, nb - 1)),
            dma((chunks, bits)),
            dma((chunks, bits)),
            dma((len(groups), nr - 1)),
            dma((len(groups), nr - 1)),
            pltpu.VMEM((2,) + pieces[0], BF16),
        ]
        + [pltpu.VMEM(piece, BF16) for piece in pieces[1:]]
        + [pltpu.VMEM(piece, BF16) for piece in pieces]
        + [pltpu.VMEM((nr, size, m), BF16) for _, size in groups],
        compiler_params=pltpu.CompilerParams(
            collective_id=0, has_side_effects=True, vmem_limit_bytes=56 << 20
        ),
        name="welch",
    )(usable_frame_tallies, retained_frequency_slots, snapshots, modes)
    out, energy = pl.pallas_call(
        write_out,
        out_shape=(
            jax.ShapeDtypeStruct((2 * share * kl, m), F32),
            jax.ShapeDtypeStruct((kl, m), F32),
        ),
        in_specs=[vmem, vmem],
        out_specs=(anywhere, anywhere),
        scratch_shapes=[dma((m // LANES + 1,))],
        name="write_out",
    )(values, energy)
    return out.reshape(share, 2, kl, m), energy


def solution(mesh):
    placed = (P("block", "row"), P(), P(), P("block", None, "row", None))
    return jax.shard_map(
        functools.partial(shards, mesh.shape["block"], mesh.shape["row"]),
        mesh=mesh,
        in_specs=placed,
        out_specs=(P("row", None, "block", None), P("block", None)),
        check_vma=False,
    )
```

profile of v0, /device:TPU:0, one launch (start us, length us, event | category | flops | bytes accessed | tf_op | source)
XLA Modules:
  0.0 46.9 jit_solution(4243867318406070907)
XLA Ops:
  0.6 44.4 %welch.1 = (f32[4,256,128]{2,1,0:T(8,128)}, f32[16,512]{1,0:T(8,128)}) custom-call(s32[64]{0:T(128)} %tally_ref.1, s32[64]{0:T(128)} %slot_ref.1, bf16[4096,128]{1,0:T(8,128)(2,1)} %snap_hbm.1, bf16[16,2,128,512]{3,2,1,0:T(8,128)(2,1)} %modes_hbm.1), custom_call_target="tpu_custom_call" | custom-call | tf_op jit(solution)/shard_map/welch/pallas_call | solution.py:349
  45.0 1.9 %write_out.1 = (f32[256,512]{1,0:T(8,128)}, f32[16,512]{1,0:T(8,128)}) custom-call(f32[4,256,128]{2,1,0:T(8,128)} %get-tuple-element.6.values_ref, f32[16,512]{1,0:T(8,128)} %get-tuple-element.7.energy_in), custom_call_target="tpu_custom_call" | custom-call | tf_op jit(solution)/shard_map/write_out/pallas_call | solution.py:384
where the time goes:
time: 47.1 us; the launch traced here: 46.9 us
  Pallas kernels  46.2 us (98%)
  between operations  0.64 us (1%)
    pallas_call x1, Pallas kernels, shards(): pl.pallas_call(functools.partial(kernel, dims), out_shape=(jax.ShapeDtype...  44.4 us
    pallas_call x1, Pallas kernels, shards(): pl.pallas_call(write_out, out_shape=(jax.ShapeDtypeStruct((2 * share * kl...  1.88 us

commit v1 on v0

--- a/solution.py
+++ b/solution.py
@@ -377,10 +377,10 @@
         + [pltpu.VMEM(piece, BF16) for piece in pieces]
         + [pltpu.VMEM((nr, size, m), BF16) for _, size in groups],
         compiler_params=pltpu.CompilerParams(
-            collective_id=0, has_side_effects=True, vmem_limit_bytes=56 << 20
+            collective_id=0, has_side_effects=True, vmem_limit_bytes=24 << 20
         ),
         name="welch",
-    )(usable_frame_tallies, retained_frequency_slots, snapshots, modes)
+    )(pltpu.with_memory_space_constraint(usable_frame_tallies, pltpu.HBM), pltpu.with_memory_space_constraint(retained_frequency_slots, pltpu.HBM), pltpu.with_memory_space_constraint(snapshots, pltpu.HBM), pltpu.with_memory_space_constraint(modes, pltpu.HBM))
     out, energy = pl.pallas_call(
         write_out,
         out_shape=(
@@ -390,6 +390,7 @@
         in_specs=[vmem, vmem],
         out_specs=(anywhere, anywhere),
         scratch_shapes=[dma((m // LANES + 1,))],
+        compiler_params=pltpu.CompilerParams(vmem_limit_bytes=1 << 20),
         name="write_out",
     )(values, energy)
     return out.reshape(share, 2, kl, m), energy

time: 47.1 us -> 45.2 us (0.960)
  Pallas kernels: 46.2 us -> 44.4 us
    pallas_call x1, Pallas kernels: 1.88 us -> 0.84 us  [shards(): pl.pallas_call(write_out, out_shape=(jax.ShapeDtypeStruct((2 * share * kl...]
    pallas_call x1, Pallas kernels: 44.4 us -> 43.6 us  [shards(): pl.pallas_call(functools.partial(kernel, dims), out_shape=(jax.ShapeDtype...]
where the time goes in v1:
time: 45.2 us; the launch traced here: 45 us
  Pallas kernels  44.4 us (98%)
  between operations  0.64 us (1%)
    pallas_call x1, Pallas kernels, shards(): pl.pallas_call(functools.partial(kernel, dims), out_shape=(jax.ShapeDtype...  43.6 us

profile of v1, /device:TPU:0, one launch (start us, length us, event | category | flops | bytes accessed | tf_op | source)
XLA Modules:
  0.0 45.0 jit_solution(14397166666668563597)
XLA Ops:
  0.6 43.6 %welch.1 = (f32[4,256,128]{2,1,0:T(8,128)S(1)}, f32[16,512]{1,0:T(8,128)S(1)}) custom-call(s32[64]{0:T(128)} %tally_ref.1, s32[64]{0:T(128)} %slot_ref.1, bf16[4096,128]{1,0:T(8,128)(2,1)} %snap_hbm.1, bf16[16,2,128,512]{3,2,1,0:T(8,128)(2,1)} %modes_hbm.1), custom_call_target="tpu_custom_call" | custom-call | tf_op jit(solution)/shard_map/welch/pallas_call | solution.py:349
  44.2 0.8 %write_out.1 = (f32[256,512]{1,0:T(8,128)}, f32[16,512]{1,0:T(8,128)}) custom-call(f32[4,256,128]{2,1,0:T(8,128)S(1)} %get-tuple-element.6.values_ref, f32[16,512]{1,0:T(8,128)S(1)} %get-tuple-element.7.energy_in), custom_call_target="tpu_custom_call" | custom-call | tf_op jit(solution)/shard_map/write_out/pallas_call | solution.py:384
